TPU v7x, 32 devices: a whole 2x2x4 slice. The times are simulated.
32 devices in a mesh: aux: 4 (over z), pair: 8 (over y, x, core).
Axes of the slice: x: 2, y: 2, z: 4, core: 2. Of those that a mesh axis runs over, the one named last changes fastest.
Arguments:
- b_three: bfloat16 [4096, 2048], P('pair', 'aux'), may hold values from -0.13183594 to 0.13183594
- metric: bfloat16 [2048, 2048], P(None, 'aux'), may hold values from -1 to 2
- aux_map: int32 [64, 32], P('pair', 'aux'), may hold values 0 or 1
- domains: int32 [80, 4], replicated, may hold values from 0 to 63, as said below
- counts: int32 [80], P('pair'), may hold values from 1 to 4, as said below
Outputs:
- pair_integrals: float32 [80, 256, 256], P('pair', 'aux')
Inputs may be any that keep to these rules, and one draw needn't show every extreme that they name: `domains`: of the 40 slots of the pairs of one index of pair (pairs q * 10 to (q + 1) * 10 - 1), at most 5 name blocks held by one index of pair (blocks o * 8 to (o + 1) * 8 - 1), and exactly 5 for some such index in every draw. `counts`: slots at or past a pair's count are padding.
All inputs are finite; a program needn't handle non-finite values. No bound on the sum of `aux_map` on one device may be relied on, other than what follows from the above.
Results may differ from a plain program's by a relative error of at most 0.00079.
Values may be sent and summed in bfloat16 or wider, within the bound.
A program may use at most 64 MiB of HBM per device.

v0:
```python
import jax
import jax.numpy as jnp
from jax import lax
from jax.sharding import PartitionSpec as P


def per_device(b_three, metric, aux_map, domains, counts):
    rows_dev, aux_dev = b_three.shape
    blocks_dev, aux_blocks = aux_map.shape
    width_cw = rows_dev // blocks_dev
    aux_width = aux_dev // aux_blocks
    keep_mask = aux_map.astype(jnp.bfloat16)
    masked = (
        b_three.reshape(blocks_dev, width_cw, aux_blocks, aux_width) * keep_mask[:, None, :, None]
    ).reshape(rows_dev, aux_dev)
    fitted = jnp.dot(
        lax.all_gather(masked, "aux", axis=1, tiled=True),
        metric,
        preferred_element_type=jnp.float32,
    ).astype(jnp.bfloat16)
    block_table = fitted.reshape(blocks_dev, width_cw * aux_dev)
    peer_count = lax.axis_size("pair")
    own_index = lax.axis_index("pair")
    pairs_dev = counts.shape[0]
    domain_max = domains.shape[1]
    slot_count = pairs_dev * domain_max
    all_domains = domains.reshape(peer_count, slot_count)
    own_domains = lax.dynamic_slice_in_dim(all_domains, own_index, 1, 0)[0]
    shard_piece = lax.all_gather(block_table, "pair", axis=0, tiled=True)
    block_ids = jnp.arange(shard_piece.shape[0], dtype=jnp.int32)
    onehot = (own_domains[:, None] == block_ids[None, :]).astype(jnp.bfloat16)
    chosen = jnp.dot(onehot, shard_piece, preferred_element_type=jnp.float32).astype(jnp.bfloat16)
    stacks = chosen.reshape(pairs_dev, domain_max * width_cw, aux_dev)
    partial_value = jnp.einsum("pax,pbx->pab", stacks, stacks, preferred_element_type=jnp.float32)
    slot_of = jnp.arange(domain_max * width_cw, dtype=jnp.int32) // width_cw
    live_rows = slot_of[None, :] < counts[:, None]
    partial_value = jnp.where(
        live_rows[:, :, None] & live_rows[:, None, :], partial_value, jnp.zeros_like(partial_value)
    )
    return lax.psum_scatter(partial_value, "aux", scatter_dimension=1, tiled=True)


def solution(mesh):
    return jax.shard_map(
        per_device,
        mesh=mesh,
        in_specs=(P("pair", "aux"), P(None, "aux"), P("pair", "aux"), P(), P("pair")),
        out_specs=P("pair", "aux", None),
        check_vma=False,
    )
```

profile of v0, /device:TPU:0, one launch (start us, length us, event | category | flops | bytes accessed | tf_op | source)
XLA Modules:
  0.0 172.9 jit_solution(9193353961309677917)
XLA Ops:
  6.5 0.0 copy-start
  6.5 0.0 all-gather.3.cloned.1.call-start
  6.5 0.8 convert_element_type.10
  7.4 0.2 mul.11
  7.6 1.4 mul.12
  9.0 2.1 %mul.13 = bf16[512,512]{1,0:T(8,128)(2,1)} multiply(bf16[512,512]{1,0:T(8,128)(2,1)} %param.5, bf16[512,512]{1,0:T(8,128)(2,1)} %mul.12) | non-fusion elementwise | flops 262144 | bytes 1572864 | tf_op jit(solution)/shard_map/mul | solution.py:14
  11.1 0.0 all-gather.3.cloned.1.call-update
  11.1 0.0 copy-start.1
  11.2 0.0 copy-start.2
  11.2 0.0 all-gather.5.cloned.1.call-start
  11.2 48.5 %all-gather.3.cloned.1.call-done = bf16[512,2048]{1,0:T(8,128)(2,1)} async-done(((bf16[512,512]{1,0:T(8,128)(2,1)}), bf16[512,2048]{1,0:T(8,128)(2,1)}) %all-gather.3.cloned.1.call-update) | async-done | bytes 2097168 | tf_op jit(solution)/shard_map/all_gather | solution.py:17
  59.7 0.0 copy-done
  59.7 2.8 %convolution_convert_fusion.1 = bf16[512,512]{1,0:T(8,128)(2,1)S(1)} fusion(bf16[512,2048]{1,0:T(8,128)(2,1)} %all-gather.3.cloned.1.call-done, bf16[2048,512]{1,0:T(8,128)(2,1)S(1)} %copy-done), kind=kOutput, calls=%fused_computation.2 | convolution fusion | flops 1074003968 | bytes 4718592 | tf_op jit(solution)/shard_map/dot_general | solution.py:16
  62.5 1.0 reshape.77
  63.6 0.0 all-gather.5.cloned.1.call-update
  63.6 0.0 reduce-scatter.2.cloned.1.call-start
  63.6 0.0 copy-done.1
  63.6 0.1 copy.6
  63.7 0.1 reshape.76
  63.8 0.0 copy-done.2
  63.9 0.1 broadcast_compare_fusion
  63.9 35.2 %all-gather.5.cloned.1.call-done = bf16[64,32768]{1,0:T(8,128)(2,1)} async-done(((bf16[8,32768]{1,0:T(8,128)(2,1)}), bf16[64,32768]{1,0:T(8,128)(2,1)}) %all-gather.5.cloned.1.call-update) | async-done | bytes 4194320 | tf_op jit(solution)/shard_map/all_gather | solution.py:29
  99.1 4.6 %convolution_convert_fusion = bf16[40,32768]{1,0:T(8,128)(2,1)} fusion(bf16[64,32768]{1,0:T(8,128)(2,1)} %all-gather.5.cloned.1.call-done, s32[40]{0:T(128)S(1)} %dynamic-slice_bitcast_fusion), kind=kOutput, calls=%fused_computation | convolution fusion | flops 169085440 | bytes 6815904 | tf_op jit(solution)/shard_map/dot_general | solution.py:32
  103.7 5.3 %reshape.78 = bf16[10,256,512]{2,1,0:T(8,128)(2,1)} reshape(bf16[40,32768]{1,0:T(8,128)(2,1)} %convolution_convert_fusion) | data formatting | bytes 5242880 | tf_op jit(solution)/shard_map/reshape | solution.py:33
  109.0 5.0 %and_select_fusion = f32[10,256,256]{2,1,0:T(8,128)} fusion(bf16[10,256,512]{2,1,0:T(8,128)(2,1)} %reshape.78, pred[10,256]{1,0:T(8,128)(4,1)S(1)} %broadcast_compare_fusion), kind=kOutput, calls=%fused_computation.1 | convolution fusion | flops 672399360 | bytes 5245440 | tf_op jit(solution)/shard_map/pax,pbx->pab/dot_general | solution.py:34
  114.0 0.0 reduce-scatter.2.cloned.1.call-update
  114.0 52.4 %reduce-scatter.2.cloned.1.call-done = f32[10,64,256]{2,1,0:T(8,128)} async-done(((f32[10,256,256]{2,1,0:T(8,128)}), f32[10,64,256]{2,1,0:T(8,128)}) %reduce-scatter.2.cloned.1.call-update) | async-done | bytes 655376 | tf_op jit(solution)/shard_map/reduce_scatter | solution.py:40
  (2 shorter events, 0.0 us)
Async XLA Ops:
  6.5 53.1 %copy-start = (bf16[2048,512]{1,0:T(8,128)(2,1)S(1)}, bf16[2048,512]{1,0:T(8,128)(2,1)}, u32[]{:S(2)}) copy-start(bf16[2048,512]{1,0:T(8,128)(2,1)} %param.6) | copy-start | bytes 6291460
  6.5 53.1 %all-gather.3.cloned.1.call-start = ((), (), s32[]{:S(2)}) async-start(), calls=%async_computation.1 | async-start | bytes 2621440 | tf_op jit(solution)/shard_map/all_gather | solution.py:17
  11.1 52.5 %copy-start.1 = (s32[80,4]{0,1:T(4,128)S(1)}, s32[80,4]{0,1:T(4,128)}, u32[]{:S(2)}) copy-start(s32[80,4]{0,1:T(4,128)} %param.8) | copy-start | bytes 3844
  11.2 52.7 %copy-start.2 = (s32[10]{0:T(128)S(1)}, s32[10]{0:T(128)}, u32[]{:S(2)}) copy-start(s32[10]{0:T(128)} %param.9) | copy-start | bytes 124
  11.2 88.0 %all-gather.5.cloned.1.call-start = ((), (), s32[]{:S(2)}) async-start(), calls=%async_computation.2 | async-start | bytes 4718592 | tf_op jit(solution)/shard_map/all_gather | solution.py:29
  63.6 102.8 %reduce-scatter.2.cloned.1.call-start = ((), (), s32[]{:S(2)}) async-start(), calls=%async_computation.3 | async-start | bytes 3276800 | tf_op jit(solution)/shard_map/reduce_scatter | solution.py:40
Sparse Core Ops, SparseCore 0:
  11.3 48.3 all-gather.2
  63.7 35.3 all-gather.4
  114.1 52.2 reduce-scatter.1
where the time goes:
time: 173 us
  waiting for transfers between devices  136 us (79%)
  between operations  13.2 us (8%)
  matrix products  12.4 us (7%)
  local copies, waits for them, and re-layouts  8.12 us (5%)
  other arithmetic  3.04 us (2%)
    reduce_scatter x1, waiting for transfers between devices, per_device(): lax.psum_scatter(partial_value, 'aux', scatter_dimension=1, tiled=True)  52.4 us
    all_gather x1, waiting for transfers between devices, per_device(): lax.all_gather(masked, 'aux', axis=1, tiled=True)  48.5 us
    all_gather x1, waiting for transfers between devices, per_device(): shard_piece = lax.all_gather(block_table, 'pair', axis=0, tiled=True)  35.2 us
    reshape x1, local copies, waits for them, and re-layouts, per_device(): stacks = chosen.reshape(pairs_dev, domain_max * width_cw, aux_dev)  5.27 us
    dot_general x1, matrix products, per_device(): jnp.einsum('pax,pbx->pab', stacks, stacks, preferred_element_type=jnp.flo...  4.97 us
    dot_general x1, matrix products, per_device(): jnp.dot(onehot, shard_piece, preferred_element_type=jnp.float32)  4.62 us
  transfers between devices with their start and end apart: 3, of which 3 were waited for; matrix products, arithmetic and copies ran while one was open for 0% of the time, Pallas kernels for 0%

commit v1 on v0

--- a/solution.py
+++ b/solution.py
@@ -2,6 +2,17 @@
 import jax.numpy as jnp
 from jax import lax
 from jax.sharding import PartitionSpec as P
+
+
+def collect(x, axis, dim):
+    ways = lax.axis_size(axis)
+    pieces = [x]
+    for far in range(1, ways):
+        pieces.append(
+            lax.ppermute(pieces[far - 1], axis, [(d, (d - 1) % ways) for d in range(ways)])
+        )
+    line = jnp.concatenate(pieces, axis=dim)
+    return jnp.roll(line, lax.axis_index(axis) * x.shape[dim], axis=dim)
 
 
 def per_device(b_three, metric, aux_map, domains, counts):
@@ -13,11 +24,9 @@
     masked = (
         b_three.reshape(blocks_dev, width_cw, aux_blocks, aux_width) * keep_mask[:, None, :, None]
     ).reshape(rows_dev, aux_dev)
-    fitted = jnp.dot(
-        lax.all_gather(masked, "aux", axis=1, tiled=True),
-        metric,
-        preferred_element_type=jnp.float32,
-    ).astype(jnp.bfloat16)
+    fitted = jnp.dot(collect(masked, "aux", 1), metric, preferred_element_type=jnp.float32).astype(
+        jnp.bfloat16
+    )
     block_table = fitted.reshape(blocks_dev, width_cw * aux_dev)
     peer_count = lax.axis_size("pair")
     own_index = lax.axis_index("pair")

time: 173 us -> 181 us (1.046)
  waiting for transfers between devices: 136 us -> 120 us
  starting transfers between devices: 0.09 us -> 13.7 us
  local copies, waits for them, and re-layouts: 8.12 us -> 17.4 us
    all_gather x1 -> x0, waiting for transfers between devices: 48.5 us -> none  [per_device(): lax.all_gather(masked, 'aux', axis=1, tiled=True)]
    ppermute x0 -> x3, waiting for transfers between devices: none -> 29.2 us  [collect(): lax.ppermute(pieces[far - 1], axis, [(d, (d - 1) % ways) for d in range(w...]
    ppermute x0 -> x3, starting transfers between devices: none -> 13.6 us  [collect(): lax.ppermute(pieces[far - 1], axis, [(d, (d - 1) % ways) for d in range(w...]
    unnamed x7 -> x15, local copies, waits for them, and re-layouts: 0.12 us -> 7.55 us
    all_gather x1, waiting for transfers between devices: 35.2 us -> 38.4 us  [per_device(): shard_piece = lax.all_gather(block_table, 'pair', axis=0, tiled=True)]
    unnamed x0 -> x1, other arithmetic: none -> 2.21 us
    mul x1 -> x0, other arithmetic: 2.12 us -> none  [per_device(): b_three.reshape(blocks_dev, width_cw, aux_blocks, aux_width)]
    concatenate x0 -> x1, local copies, waits for them, and re-layouts: none -> 1.91 us  [collect(): return jnp.roll(line, lax.axis_index(axis) * x.shape[dim], axis=dim)]
  transfers between devices with their start and end apart: 3 -> 5, of which waited for: 3 -> 5; matrix products, arithmetic and copies ran while one was open for 0% -> 1% of each run, Pallas kernels for 0% -> 0%
where the time goes in v1:
time: 181 us; the launch traced here: 180 us
  waiting for transfers between devices  120 us (66%)
  local copies, waits for them, and re-layouts  17.4 us (10%)
  starting transfers between devices  13.7 us (8%)
  between operations  13.5 us (7%)
  matrix products  12.5 us (7%)
  other arithmetic  3.12 us (2%)
    reduce_scatter x1, waiting for transfers between devices, per_device(): lax.psum_scatter(partial_value, 'aux', scatter_dimension=1, tiled=True)  52.4 us
    all_gather x1, waiting for transfers between devices, per_device(): shard_piece = lax.all_gather(block_table, 'pair', axis=0, tiled=True)  38.4 us
    ppermute x3, waiting for transfers between devices, collect(): lax.ppermute(pieces[far - 1], axis, [(d, (d - 1) % ways) for d in range(w...  29.2 us
    ppermute x3, starting transfers between devices, collect(): lax.ppermute(pieces[far - 1], axis, [(d, (d - 1) % ways) for d in range(w...  13.6 us
    unnamed x15, local copies, waits for them, and re-layouts  7.55 us
    reshape x1, local copies, waits for them, and re-layouts, per_device(): stacks = chosen.reshape(pairs_dev, domain_max * width_cw, aux_dev)  5.25 us
    dot_general x1, matrix products, per_device(): jnp.einsum('pax,pbx->pab', stacks, stacks, preferred_element_type=jnp.flo...  4.97 us
    dot_general x1, matrix products, per_device(): jnp.dot(onehot, shard_piece, preferred_element_type=jnp.float32)  4.62 us
  transfers between devices with their start and end apart: 5, of which 5 were waited for; matrix products, arithmetic and copies ran while one was open for 1% of the time, Pallas kernels for 0%

profile of v1, /device:TPU:0, one launch (start us, length us, event | category | flops | bytes accessed | tf_op | source)
XLA Modules:
  0.0 180.2 jit_solution(1801180953366673909)
XLA Ops:
  6.5 0.0 copy-start
  6.5 0.0 all-gather.2.cloned.1.call-start
  6.5 0.8 convert_element_type.10
  7.4 0.2 mul.14
  7.6 1.4 mul.15
  9.0 2.2 %constant_dynamic-update-slice_fusion.7 = (bf16[512,4096]{1,0:T(8,128)(2,1)}, bf16[512,512]{1,0:T(8,128)(2,1)S(1)}) fusion(bf16[512,512]{1,0:T(8,128)(2,1)} %param.5, bf16[512,512]{1,0:T(8,128)(2,1)} %mul.15), kind=kLoop, calls=%fused_computation.13 | loop fusion | flops 1048575 | bytes 2097152
  11.2 0.0 copy-start.1
  11.2 5.1 %collective-permute-start = (bf16[512,512]{1,0:T(8,128)(2,1)S(1)}, bf16[512,512]{1,0:T(8,128)(2,1)S(1)}, u32[]{:S(2)}, u32[]{:S(2)}) collective-permute-start(bf16[512,512]{1,0:T(8,128)(2,1)S(1)} %get-tuple-element.6), channel_id=1, source_target_pairs={{0,24},{8,0},{16,8},{24,16},{1,25},{9,1},{17,9},{25,17},{2,26},{10... | collective-permute-start | bytes 1572872 | tf_op jit(solution)/shard_map/ppermute | solution.py:12
  16.3 11.2 %collective-permute-done = bf16[512,512]{1,0:T(8,128)(2,1)S(1)} collective-permute-done((bf16[512,512]{1,0:T(8,128)(2,1)S(1)}, bf16[512,512]{1,0:T(8,128)(2,1)S(1)}, u32[]{:S(2)}, u32[]{:S(2)}) %collective-permute-start) | collective-permute-done | bytes 524320 | tf_op jit(solution)/shard_map/ppermute | solution.py:12
  27.5 4.3 %collective-permute-start.1 = (bf16[512,512]{1,0:T(8,128)(2,1)S(1)}, bf16[512,512]{1,0:T(8,128)(2,1)S(1)}, u32[]{:S(2)}, u32[]{:S(2)}) collective-permute-start(bf16[512,512]{1,0:T(8,128)(2,1)S(1)} %collective-permute-done), channel_id=1, source_target_pairs={{0,24},{8,0},{16,8},{24,16},{1,25},{9,1},{17,9},{25,17},{2,26},{10... | collective-permute-start | bytes 1572872 | tf_op jit(solution)/shard_map/ppermute | solution.py:12
  31.7 10.3 %collective-permute-done.1 = bf16[512,512]{1,0:T(8,128)(2,1)S(1)} collective-permute-done((bf16[512,512]{1,0:T(8,128)(2,1)S(1)}, bf16[512,512]{1,0:T(8,128)(2,1)S(1)}, u32[]{:S(2)}, u32[]{:S(2)}) %collective-permute-start.1) | collective-permute-done | bytes 524320 | tf_op jit(solution)/shard_map/ppermute | solution.py:12
  42.1 0.0 copy-done.1
  42.1 4.3 %collective-permute-start.2 = (bf16[512,512]{1,0:T(8,128)(2,1)S(1)}, bf16[512,512]{1,0:T(8,128)(2,1)}, u32[]{:S(2)}, u32[]{:S(2)}) collective-permute-start(bf16[512,512]{1,0:T(8,128)(2,1)S(1)} %collective-permute-done.1), channel_id=1, source_target_pairs={{0,24},{8,0},{16,8},{24,16},{1,25},{9,1},{17,9},{25,17},{2,26},{10... | collective-permute-start | bytes 1572872 | tf_op jit(solution)/shard_map/ppermute | solution.py:12
  46.4 0.9 constant_dynamic-update-slice_fusion.6
  47.2 0.9 constant_dynamic-update-slice_fusion.5
  48.1 7.7 %collective-permute-done.2 = bf16[512,512]{1,0:T(8,128)(2,1)} collective-permute-done((bf16[512,512]{1,0:T(8,128)(2,1)S(1)}, bf16[512,512]{1,0:T(8,128)(2,1)}, u32[]{:S(2)}, u32[]{:S(2)}) %collective-permute-start.2) | collective-permute-done | bytes 524320 | tf_op jit(solution)/shard_map/ppermute | solution.py:12
  55.8 2.0 %constant_dynamic-update-slice_fusion.4 = bf16[512,4096]{1,0:T(8,128)(2,1)} fusion(bf16[512,4096]{1,0:T(8,128)(2,1)} %constant_dynamic-update-slice_fusion.5, bf16[512,512]{1,0:T(8,128)(2,1)} %collective-permute-done.2), kind=kLoop, calls=%fused_computation.10 | loop fusion | bytes 1048576
  57.8 2.0 %constant_dynamic-update-slice_fusion.3 = bf16[512,4096]{1,0:T(8,128)(2,1)} fusion(bf16[512,4096]{1,0:T(8,128)(2,1)} %constant_dynamic-update-slice_fusion.4, bf16[512,512]{1,0:T(8,128)(2,1)} %copy-done.1), kind=kLoop, calls=%fused_computation.9 | loop fusion | bytes 1048576
  59.8 0.9 constant_dynamic-update-slice_fusion.2
  60.6 0.9 constant_dynamic-update-slice_fusion.1
  61.5 1.9 %constant_dynamic-update-slice_fusion = bf16[512,4096]{1,0:T(8,128)(2,1)} fusion(bf16[512,4096]{1,0:T(8,128)(2,1)} %constant_dynamic-update-slice_fusion.1, bf16[512,512]{1,0:T(8,128)(2,1)} %collective-permute-done.2), kind=kLoop, calls=%fused_computation.6 | loop fusion | bytes 1048576 | tf_op jit(solution)/shard_map/jit(_roll_dynamic)/concatenate | solution.py:15
  63.4 0.0 copy-done
  63.4 0.0 copy-start.2
  63.4 0.0 copy-start.3
  63.4 2.9 %fusion.2 = bf16[512,512]{1,0:T(8,128)(2,1)S(1)} fusion(bf16[2048,512]{1,0:T(8,128)(2,1)S(1)} %copy-done, bf16[512,4096]{1,0:T(8,128)(2,1)} %constant_dynamic-update-slice_fusion, s32[]{:T(128)S(6)} %select_n.32), kind=kOutput, calls=%fused_computation.4 | convolution fusion | flops 1074003968 | bytes 4718596 | tf_op jit(solution)/shard_map/dot_general | solution.py:27
  66.3 1.0 reshape.77
  67.3 0.0 all-gather.2.cloned.1.call-update
  67.3 0.0 reduce-scatter.2.cloned.1.call-start
  67.4 0.0 copy-done.2
  67.4 0.1 copy.6
  67.5 0.1 reshape.76
  67.6 0.0 copy-done.3
  67.6 0.1 broadcast_compare_fusion
  67.7 38.4 %all-gather.2.cloned.1.call-done = bf16[64,32768]{1,0:T(8,128)(2,1)} async-done(((bf16[8,32768]{1,0:T(8,128)(2,1)}), bf16[64,32768]{1,0:T(8,128)(2,1)}) %all-gather.2.cloned.1.call-update) | async-done | bytes 4194320 | tf_op jit(solution)/shard_map/all_gather | solution.py:38
  106.1 4.6 %convolution_convert_fusion = bf16[40,32768]{1,0:T(8,128)(2,1)} fusion(bf16[64,32768]{1,0:T(8,128)(2,1)} %all-gather.2.cloned.1.call-done, s32[40]{0:T(128)S(1)} %dynamic-slice_bitcast_fusion), kind=kOutput, calls=%fused_computation | convolution fusion | flops 169085440 | bytes 6815904 | tf_op jit(solution)/shard_map/dot_general | solution.py:41
  110.7 5.3 %reshape.78 = bf16[10,256,512]{2,1,0:T(8,128)(2,1)} reshape(bf16[40,32768]{1,0:T(8,128)(2,1)} %convolution_convert_fusion) | data formatting | bytes 5242880 | tf_op jit(solution)/shard_map/reshape | solution.py:42
  116.0 5.0 %and_select_fusion = f32[10,256,256]{2,1,0:T(8,128)} fusion(bf16[10,256,512]{2,1,0:T(8,128)(2,1)} %reshape.78, pred[10,256]{1,0:T(8,128)(4,1)S(1)} %broadcast_compare_fusion), kind=kOutput, calls=%fused_computation.1 | convolution fusion | flops 672399360 | bytes 5245440 | tf_op jit(solution)/shard_map/pax,pbx->pab/dot_general | solution.py:43
  120.9 0.0 reduce-scatter.2.cloned.1.call-update
  121.0 52.4 %reduce-scatter.2.cloned.1.call-done = f32[10,64,256]{2,1,0:T(8,128)} async-done(((f32[10,256,256]{2,1,0:T(8,128)}), f32[10,64,256]{2,1,0:T(8,128)}) %reduce-scatter.2.cloned.1.call-update) | async-done | bytes 655376 | tf_op jit(solution)/shard_map/reduce_scatter | solution.py:49
  (2 shorter events, 0.0 us)
Async XLA Ops:
  6.5 56.9 %copy-start = (bf16[2048,512]{1,0:T(8,128)(2,1)S(1)}, bf16[2048,512]{1,0:T(8,128)(2,1)}, u32[]{:S(2)}) copy-start(bf16[2048,512]{1,0:T(8,128)(2,1)} %param.6) | copy-start | bytes 6291460
  6.5 99.6 %all-gather.2.cloned.1.call-start = ((), (), s32[]{:S(2)}) async-start(), calls=%async_computation.1 | async-start | bytes 4718592 | tf_op jit(solution)/shard_map/all_gather | solution.py:38
  11.2 30.9 %copy-start.1 = (bf16[512,512]{1,0:T(8,128)(2,1)}, bf16[512,512]{1,0:T(8,128)(2,1)S(1)}, u32[]{:S(2)}) copy-start(bf16[512,512]{1,0:T(8,128)(2,1)S(1)} %get-tuple-element.6) | copy-start | bytes 1572868
  11.2 16.3 %collective-permute-start = (bf16[512,512]{1,0:T(8,128)(2,1)S(1)}, bf16[512,512]{1,0:T(8,128)(2,1)S(1)}, u32[]{:S(2)}, u32[]{:S(2)}) collective-permute-start(bf16[512,512]{1,0:T(8,128)(2,1)S(1)} %get-tuple-element.6), channel_id=1, source_target_pairs={{0,24},{8,0},{16,8},{24,16},{1,25},{9,1},{17,9},{25,17},{2,26},{10... | collective-permute-start | bytes 1572872 | tf_op jit(solution)/shard_map/ppermute | solution.py:12
  27.5 14.6 %collective-permute-start.1 = (bf16[512,512]{1,0:T(8,128)(2,1)S(1)}, bf16[512,512]{1,0:T(8,128)(2,1)S(1)}, u32[]{:S(2)}, u32[]{:S(2)}) collective-permute-start(bf16[512,512]{1,0:T(8,128)(2,1)S(1)} %collective-permute-done), channel_id=1, source_target_pairs={{0,24},{8,0},{16,8},{24,16},{1,25},{9,1},{17,9},{25,17},{2,26},{10... | collective-permute-start | bytes 1572872 | tf_op jit(solution)/shard_map/ppermute | solution.py:12
  42.1 13.8 %collective-permute-start.2 = (bf16[512,512]{1,0:T(8,128)(2,1)S(1)}, bf16[512,512]{1,0:T(8,128)(2,1)}, u32[]{:S(2)}, u32[]{:S(2)}) collective-permute-start(bf16[512,512]{1,0:T(8,128)(2,1)S(1)} %collective-permute-done.1), channel_id=1, source_target_pairs={{0,24},{8,0},{16,8},{24,16},{1,25},{9,1},{17,9},{25,17},{2,26},{10... | collective-permute-start | bytes 1572872 | tf_op jit(solution)/shard_map/ppermute | solution.py:12
  63.4 4.0 %copy-start.2 = (s32[80,4]{0,1:T(4,128)S(1)}, s32[80,4]{0,1:T(4,128)}, u32[]{:S(2)}) copy-start(s32[80,4]{0,1:T(4,128)} %param.8) | copy-start | bytes 3844
  63.4 4.2 %copy-start.3 = (s32[10]{0:T(128)S(1)}, s32[10]{0:T(128)}, u32[]{:S(2)}) copy-start(s32[10]{0:T(128)} %param.9) | copy-start | bytes 124
  67.3 106.1 %reduce-scatter.2.cloned.1.call-start = ((), (), s32[]{:S(2)}) async-start(), calls=%async_computation.2 | async-start | bytes 3276800 | tf_op jit(solution)/shard_map/reduce_scatter | solution.py:49
Sparse Core Ops, SparseCore 0:
  67.4 38.6 all-gather.1
  121.1 52.2 reduce-scatter.1
